TPU v7x, 32 devices: a whole 2x2x4 slice. The times are simulated.
32 devices in a mesh: lat: 4 (over z), lon: 8 (over y, x, core).
Axes of the slice: x: 2, y: 2, z: 4, core: 2. Of those that a mesh axis runs over, the one named last changes fastest.
Arguments:
- inputs: bfloat16 [128, 360, 512], P('lat', 'lon'), may hold values from -6 to 6
- metric: float32 [128, 360], P('lat', 'lon'), may hold values from 0.5 to 2
- kernel_one: float32 [9, 512], replicated, may hold values from -2 to 2
- kernel_two: float32 [9, 512], replicated, may hold values from -2 to 2
- widths: int32 [128], P('lat'), may hold values from 0 to 90, as said below
- zonal_gains: bfloat16 [128, 181], P('lat'), may hold values from -0.19921875 to 0.19921875
- norm_gain: float32 [512], replicated, may hold values from 0.5 to 1.5
- weight_in: bfloat16 [512, 1024], replicated, may hold values from -0.25 to 0.25
- weight_out: bfloat16 [1024, 512], replicated, may hold values from -0.1875 to 0.1875
Outputs:
- updated: bfloat16 [128, 360, 512], P('lat', 'lon')
Inputs may be any that keep to these rules, and one draw needn't show every extreme that they name: widths gives the zonal filter half-width of each latitude row.
All inputs are finite; a program needn't handle non-finite values.
Results may differ from a plain program's by a relative error of at most 0.0061.
Values may be sent and summed in bfloat16 or wider, within the bound.
A program may use at most 64 MiB of HBM per device.

v0:
```python
import functools

import jax
import jax.numpy as jnp
from jax import lax
from jax.experimental import pallas as pl
from jax.experimental.pallas import tpu as pltpu
from jax.sharding import PartitionSpec as P

MESH = pl.DeviceIdType.MESH
LANES = 128
LEAD = 8


def round_up(value, step):
    return -(-value // step) * step


def gelu_tanh(values):
    return jax.nn.gelu(values, approximate=True)


def body(
    lats, n, rows, cols, chans, pad, reach,
    x_ref, metric_ref, k1_ref, k2_ref, widths_ref, gains_ref, gain_ref, win_hbm, wout_hbm,
    out_ref,
    ext, sec, held, acc, mix, circ, zsend, zrecv, flatx, edge, edge_in, strip, strip_in, rim, rim_in,
    taps, lines, taps_one, win_ref, wout_ref,
    w_sem,
    hs_sem, hr_sem, fs_sem, fr_sem, rs_sem, rr_sem,
):
    lat = lax.axis_index("lat")
    me = lax.axis_index("lon")
    chunks = rows // n
    half = n // 2
    wide = ext.shape[1]
    full = ext.shape[2]
    slabs = 2 * reach + 1

    at_top = lat == 0
    at_bottom = lat == lats - 1
    up_lat = jnp.where(at_top, 0, lat - 1)
    up_lon = jnp.where(at_top, lax.rem(me + half, n), me)
    down_lat = jnp.where(at_bottom, lats - 1, lat + 1)
    down_lon = jnp.where(at_bottom, lax.rem(me + half, n), me)
    left = lax.rem(me + n - 1, n)
    right = lax.rem(me + 1, n)

    def before(lon):
        return lax.rem(lon + n - 1, n)

    def after(lon):
        return lax.rem(lon + 1, n)

    loads = [
        pltpu.make_async_copy(win_hbm, win_ref, w_sem.at[0]),
        pltpu.make_async_copy(wout_hbm, wout_ref, w_sem.at[1]),
    ]
    for load in loads:
        load.start()

    barrier = pltpu.get_barrier_semaphore()
    greeted = [
        (lat, left), (lat, right),
        (up_lat, up_lon), (up_lat, before(up_lon)), (up_lat, after(up_lon)),
        (down_lat, down_lon), (down_lat, before(down_lon)), (down_lat, after(down_lon)),
    ] + [(lat, lax.rem(me + o, n)) for o in range(1, n)]
    for device in greeted:
        pl.semaphore_signal(barrier, inc=1, device_id=device, device_id_type=MESH)
    def clear(e, carry):
        ext[e, 0:LEAD, :] = jnp.zeros((LEAD, full), jnp.float32)
        return carry

    lax.fori_loop(0, rows + 4, clear, 0)

    diagonal = lax.broadcasted_iota(jnp.int32, (pad, cols), 0) == lax.broadcasted_iota(
        jnp.int32, (pad, cols), 1
    )

    for c in range(chans // LANES):
        lanes = slice(c * LANES, (c + 1) * LANES)
        flatx[c] = x_ref[:, :, lanes].astype(jnp.float32).reshape(cols * rows, LANES)

    def place(i, carry):
        line = jnp.broadcast_to(metric_ref[pl.ds(i, 1), :], (pad, cols))
        column = jnp.sum(jnp.where(diagonal, line, 0.0), axis=1, keepdims=True)
        weight = jnp.broadcast_to(column, (pad, LANES))
        ext[i + 2, pad:wide, :] = jnp.zeros((wide - pad, full), jnp.float32)
        held[i, pad - 8:pad, :] = jnp.zeros((8, chans), jnp.float32)
        ext[i + 2, LEAD:wide, chans:] = weight
        rim[0, i] = weight[0:1]
        rim[1, i] = weight[cols - 1:cols]
        for c in range(chans // LANES):
            lanes = slice(c * LANES, (c + 1) * LANES)
            cells = flatx[c, pl.ds(i, cols, stride=rows), :]
            held[i, 0:cols, lanes] = cells
            first = (cells * weight[0:cols]).astype(jnp.bfloat16).astype(jnp.float32)
            ext[i + 2, LEAD:LEAD + cols, lanes] = first
            strip[0, i, :, lanes] = first[0:2].astype(jnp.bfloat16)
            strip[1, i, :, lanes] = first[cols - 2:cols].astype(jnp.bfloat16)
        return carry

    lax.fori_loop(0, rows, place, 0)
    for slot, row in enumerate((2, 3, rows, rows + 1)):
        edge[slot] = ext[row, LEAD:wide, 0:chans].astype(jnp.bfloat16)
    pl.semaphore_wait(barrier, len(greeted))

    halo = []

    def send_halo(src, dst, recv_index, device):
        copy = pltpu.make_async_remote_copy(
            src_ref=src, dst_ref=dst, send_sem=hs_sem.at[len(halo)], recv_sem=hr_sem.at[recv_index],
            device_id=device, device_id_type=MESH,
        )
        copy.start()
        halo.append(copy)

    def slot_row(slot):
        return jnp.where(slot < 2, slot, rows + slot)

    for s, device in ((0, left), (1, right)):
        send_halo(strip.at[s], strip_in.at[1 - s, pl.ds(2, rows)], 4 + s, (lat, device))
        send_halo(rim.at[s], rim_in.at[1 - s, pl.ds(2, rows)], 6 + s, (lat, device))
    for i in range(2):
        up_slot = jnp.where(at_top, 1 - i, 2 + i)
        down_slot = jnp.where(at_bottom, 3 - i, i)
        for slot, src_row, device_lat, device_lon in (
            (up_slot, i, up_lat, up_lon),
            (down_slot, rows - 2 + i, down_lat, down_lon),
        ):
            source = i if src_row < 2 else 2 + i
            dst_row = slot_row(slot)
            target = (device_lat, device_lon)
            send_halo(edge.at[source], edge_in.at[slot], slot, target)
            corners = ((0, before(device_lon)), (1, after(device_lon)))
            for s, corner_lon in corners:
                send_halo(
                    strip.at[s, src_row], strip_in.at[1 - s, dst_row], 8 + 4 * s + slot,
                    (device_lat, corner_lon),
                )
            if src_row in (0, rows - 1):
                near = jnp.where(slot < 2, 0, 1)
                send_halo(
                    ext.at[src_row + 2, pl.ds(LEAD, pad), pl.ds(chans, LANES)],
                    ext.at[dst_row, pl.ds(LEAD, pad), pl.ds(chans, LANES)],
                    16 + near, target,
                )
                for s, corner_lon in corners:
                    send_halo(
                        rim.at[s, src_row], rim_in.at[1 - s, dst_row], 18 + 2 * s + near,
                        (device_lat, corner_lon),
                    )

    tap_lanes = taps.shape[2]
    lane_ids = lax.broadcasted_iota(jnp.int32, (pad, tap_lanes), 1)
    taps_one[0, 0:9] = k1_ref[...]
    for a in range(3):
        taps_one[1, 3 * a:3 * a + 3] = k1_ref[6 - 3 * a:9 - 3 * a, :]
    count = gains_ref.shape[1]
    center = (count - 1) // 2
    lines[...] = jnp.zeros(lines.shape, jnp.float32)
    lines[:, 0:count] = gains_ref[...].astype(jnp.float32)
    for k in range(chunks):
        line = jnp.broadcast_to(lines[pl.ds(k * n + me, 1), :], (pad, tap_lanes))
        kept = jnp.abs(lane_ids - center) <= widths_ref[k * n + me]
        line = jnp.where(kept, line, 0.0)
        shifted = pltpu.roll(line, 0, 1, stride=1, stride_axis=0)
        total = jnp.zeros((pad, tap_lanes), jnp.float32)
        for d in range(slabs):
            moved = pltpu.roll(shifted, (pad - cols) * d, 1) if d else shifted
            inside = (lane_ids >= pad * d) & (lane_ids < pad * d + cols)
            total = jnp.where(inside, moved, total)
        taps[k] = total.astype(jnp.bfloat16)

    def recv_halo(src, dst, recv_index):
        pltpu.make_async_remote_copy(
            src_ref=src, dst_ref=dst, send_sem=hs_sem.at[0], recv_sem=hr_sem.at[recv_index],
            device_id=(lat, right), device_id_type=MESH,
        ).wait_recv()

    for s in range(2):
        recv_halo(strip.at[s], strip_in.at[1 - s, pl.ds(2, rows)], 4 + s)
        recv_halo(rim.at[s], rim_in.at[1 - s, pl.ds(2, rows)], 6 + s)
        row = (1, rows + 2)[s]
        recv_halo(
            ext.at[2, pl.ds(LEAD, pad), pl.ds(chans, LANES)],
            ext.at[row, pl.ds(LEAD, pad), pl.ds(chans, LANES)], 16 + s,
        )
        for near in range(2):
            recv_halo(rim.at[s, 0], rim_in.at[1 - s, (1, rows + 2)[near]], 18 + 2 * s + near)
    for slot in range(4):
        row = slot if slot < 2 else rows + slot
        recv_halo(edge.at[0], edge_in.at[slot], slot)
        for s in range(2):
            recv_halo(strip.at[s, 0], strip_in.at[1 - s, row], 8 + 4 * s + slot)
    for copy in halo:
        copy.wait_send()

    for slot in range(4):
        row = slot if slot < 2 else rows + slot
        ext[row, LEAD:wide, 0:chans] = edge_in[slot].astype(jnp.float32)

    def join(e, carry):
        for s, at in ((0, LEAD - 2), (1, LEAD + cols)):
            ext[e, at:at + 2, 0:chans] = strip_in[s, e].astype(jnp.float32)
        return carry

    def join_rim(e, carry):
        ext[e, LEAD - 1:LEAD, chans:] = rim_in[0, e]
        ext[e, LEAD + cols:LEAD + cols + 1, chans:] = rim_in[1, e]
        return carry

    lax.fori_loop(1, rows + 3, join_rim, 0)
    lax.fori_loop(0, rows + 4, join, 0)

    def stencil(src, row, kernel, lanes):
        sums = [None, None, None]
        for a in range(3):
            line = src[row + a, :, lanes]
            for b in range(3):
                term = kernel(a, b, lanes) * line
                sums[b] = term if sums[b] is None else sums[b] + term
        return pltpu.roll(sums[0], 1, 0) + sums[1] + pltpu.roll(sums[2], wide - 1, 0)

    def second_row(p, carry):
        flip = ((p == 0) & at_top) | ((p == rows + 1) & at_bottom)
        which = jnp.where(flip, 1, 0)
        weight = ext[p + 1, :, chans:]
        for c in range(chans // LANES):
            lanes = slice(c * LANES, (c + 1) * LANES)
            value = stencil(ext, p, lambda a, b, l: taps_one[which, 3 * a + b:3 * a + b + 1, l], lanes)
            value = weight * gelu_tanh(value)
            sec[p, :, lanes] = value.astype(jnp.bfloat16).astype(jnp.float32)
        return carry

    col_ids = lax.broadcasted_iota(jnp.int32, (pad, LANES), 0)

    def mixed_row(i, carry):
        for c in range(chans // LANES):
            lanes = slice(c * LANES, (c + 1) * LANES)
            value = stencil(sec, i, lambda a, b, l: k2_ref[3 * a + b:3 * a + b + 1, l], lanes)
            value = held[i, :, lanes] + value[LEAD:, :]
            mix[i, :, lanes] = jnp.where(col_ids < cols, value, 0.0).astype(jnp.bfloat16)
        return carry

    forward = []
    for k in range(chunks):
        start = 0 if k == 0 else k * n + 2
        lax.fori_loop(start, (k + 1) * n + 2, second_row, 0)
        lax.fori_loop(k * n, (k + 1) * n, mixed_row, 0)
        for o in range(1, n):
            target = lax.rem(me + o, n)
            copy = pltpu.make_async_remote_copy(
                src_ref=mix.at[k * n + target], dst_ref=circ.at[k, me + reach],
                send_sem=fs_sem.at[k, o], recv_sem=fr_sem.at[k, o],
                device_id=(lat, target), device_id_type=MESH,
            )
            copy.start()
            forward.append(copy)
        circ[k, me + reach] = mix[k * n + me]

    for load in loads:
        load.wait()

    group = 8

    def network(g, carry):
        flat = mix[pl.ds(g * group, group)].reshape(group * pad, chans).astype(jnp.float32)
        scale = lax.rsqrt(jnp.mean(flat * flat, axis=1, keepdims=True) + 1e-06)
        normed = (flat * scale * gain_ref[...]).astype(jnp.bfloat16)
        hidden = gelu_tanh(
            jnp.dot(normed, win_ref[...], preferred_element_type=jnp.float32)
        ).astype(jnp.bfloat16)
        point = jnp.dot(hidden, wout_ref[...], preferred_element_type=jnp.float32)
        acc[pl.ds(g * group, group)] = (flat + point).reshape(group, pad, chans)
        return carry

    lax.fori_loop(0, rows // group, network, 0)

    back = []
    for k in range(chunks):
        for o in range(1, n):
            source = lax.rem(me + n - o, n)
            pltpu.make_async_remote_copy(
                src_ref=mix.at[k * n], dst_ref=circ.at[k, source + reach],
                send_sem=fs_sem.at[k, o], recv_sem=fr_sem.at[k, o],
                device_id=(lat, source), device_id_type=MESH,
            ).wait_recv()
        for e in range(reach):
            circ[k, e] = circ[k, n + e]
            circ[k, n + reach + e] = circ[k, reach + e]

        def filter_block(a, carry):
            window = circ[k, pl.ds(a, slabs)].reshape(slabs * pad, chans)
            result = jnp.dot(
                taps[k, :, 0:slabs * pad], window, preferred_element_type=jnp.float32
            )
            zsend[k * n + a] = result.astype(jnp.bfloat16)
            return carry

        lax.fori_loop(0, n, filter_block, 0, unroll=4)
        for o in range(1, n):
            target = lax.rem(me + o, n)
            copy = pltpu.make_async_remote_copy(
                src_ref=zsend.at[k * n + target], dst_ref=zrecv.at[k * n + me],
                send_sem=rs_sem.at[k, o], recv_sem=rr_sem.at[k, o],
                device_id=(lat, target), device_id_type=MESH,
            )
            copy.start()
            back.append(copy)
        zrecv[k * n + me] = zsend[k * n + me]

    for k in range(chunks):
        for o in range(1, n):
            source = lax.rem(me + n - o, n)
            pltpu.make_async_remote_copy(
                src_ref=zsend.at[k * n], dst_ref=zrecv.at[k * n + source],
                send_sem=rs_sem.at[k, o], recv_sem=rr_sem.at[k, o],
                device_id=(lat, source), device_id_type=MESH,
            ).wait_recv()

        def finish(i, carry):
            out_ref[i] = (acc[i] + zrecv[i].astype(jnp.float32)).astype(jnp.bfloat16)
            return carry

        lax.fori_loop(k * n, (k + 1) * n, finish, 0)

    for copy in forward + back:
        copy.wait_send()


def local(
    lats, n,
    inputs, metric, kernel_one, kernel_two, widths, zonal_gains, norm_gain, weight_in, weight_out
):
    rows, cols, chans = inputs.shape
    pad = round_up(cols, 16)
    wide = LEAD + pad
    full = chans + LANES
    reach = n // 4
    slabs = 2 * reach + 1
    count = zonal_gains.shape[1]
    tap_lanes = round_up(max(slabs * pad, count + pad - 1), LANES)

    chunks = rows // n
    vmem = pl.BlockSpec(memory_space=pltpu.VMEM)
    sem = pltpu.SemaphoreType.DMA
    out = pl.pallas_call(
        functools.partial(body, lats, n, rows, cols, chans, pad, reach),
        out_shape=jax.ShapeDtypeStruct((rows, pad, chans), jnp.bfloat16),
        in_specs=[vmem] * 4
        + [pl.BlockSpec(memory_space=pltpu.SMEM), vmem, vmem]
        + [pl.BlockSpec(memory_space=pl.ANY)] * 2,
        out_specs=vmem,
        scratch_shapes=[
            pltpu.VMEM((rows + 4, wide, full), jnp.float32),
            pltpu.VMEM((rows + 2, wide, chans), jnp.float32),
            pltpu.VMEM((rows, pad, chans), jnp.float32),
            pltpu.VMEM((rows, pad, chans), jnp.float32),
            pltpu.VMEM((rows, pad, chans), jnp.bfloat16),
            pltpu.VMEM((chunks, n + 2 * reach, pad, chans), jnp.bfloat16),
            pltpu.VMEM((rows, pad, chans), jnp.bfloat16),
            pltpu.VMEM((rows, pad, chans), jnp.bfloat16),
            pltpu.VMEM((chans // LANES, cols * rows, LANES), jnp.float32),
            pltpu.VMEM((4, pad, chans), jnp.bfloat16),
            pltpu.VMEM((4, pad, chans), jnp.bfloat16),
            pltpu.VMEM((2, rows, 2, chans), jnp.bfloat16),
            pltpu.VMEM((2, rows + 4, 2, chans), jnp.bfloat16),
            pltpu.VMEM((2, rows, 1, LANES), jnp.float32),
            pltpu.VMEM((2, rows + 4, 1, LANES), jnp.float32),
            pltpu.VMEM((chunks, pad, tap_lanes), jnp.bfloat16),
            pltpu.VMEM((rows, tap_lanes), jnp.float32),
            pltpu.VMEM((2, 16, chans), jnp.float32),
            pltpu.VMEM(weight_in.shape, jnp.bfloat16),
            pltpu.VMEM(weight_out.shape, jnp.bfloat16),
            sem((2,)),
            sem((22,)), sem((22,)),
            sem((chunks, n)), sem((chunks, n)), sem((chunks, n)), sem((chunks, n)),
        ],
        compiler_params=pltpu.CompilerParams(
            collective_id=0, has_side_effects=True, vmem_limit_bytes=60 * 2**20
        ),
    )(
        inputs.transpose(1, 0, 2), metric, kernel_one, kernel_two, widths, zonal_gains, norm_gain.reshape(1, chans),
        weight_in, weight_out,
    )
    return out[:, :cols]


def solution(mesh):
    placed = (
        P("lat", "lon", None),
        P("lat", "lon"),
        P(),
        P(),
        P("lat"),
        P("lat", None),
        P(),
        P(),
        P(),
    )
    return jax.shard_map(
        functools.partial(local, mesh.shape["lat"], mesh.shape["lon"]),
        mesh=mesh, in_specs=placed, out_specs=P("lat", "lon", None), check_vma=False,
    )
```

profile of v0, /device:TPU:0, one launch (start us, length us, event | category | flops | bytes accessed | tf_op | source)
XLA Modules:
  0.0 57.9 jit_solution(13356090287612997143)
XLA Ops:
  0.0 54.5 %shard_map.91 = bf16[32,48,512]{2,1,0:T(8,128)(2,1)} custom-call(bf16[45,32,512]{2,1,0:T(8,128)(2,1)} %bitcast.4, f32[32,45]{1,0:T(8,128)} %metric_ref.1, f32[9,512]{1,0:T(8,128)} %k1_ref.1, f32[9,512]{1,0:T(8,128)} %k2_ref.1, s32[32]{0:T(128)} %widths_ref.1, bf16[32,181]{1,0:T(8,128)(2,1)} %gains_ref.1, f32[1,512]{1,0:T(1,128)} %bitcast.5, ...), custom_call_target="tpu_custom_call" | custom-call | tf_op jit(solution)/shard_map/pallas_call | solution.py:348
  54.5 3.3 %copy.10 = bf16[32,45,512]{2,0,1:T(8,128)(2,1)} copy(bf16[32,45,512]{2,1,0:T(8,128)(2,1)} %bitcast.3) | data formatting | bytes 2949120 | tf_op jit(solution)/shard_map/slice | solution.py:387
where the time goes:
time: 58 us; the launch traced here: 57.9 us
  Pallas kernels  54.5 us (94%)
  local copies, waits for them, and re-layouts  3.35 us (6%)
    pallas_call x1, Pallas kernels, local(): pl.pallas_call(functools.partial(body, lats, n, rows, cols, chans, pad, r...  54.5 us
    slice x1, local copies, waits for them, and re-layouts, local(): return out[:, :cols]  3.35 us

commit v1 on v0

v1 whole, which is shorter than its diff:
```python
import functools

import jax
import jax.numpy as jnp
from jax import lax
from jax.experimental import pallas as pl
from jax.experimental.pallas import tpu as pltpu
from jax.sharding import PartitionSpec as P

MESH = pl.DeviceIdType.MESH
LANES = 128
LEAD = 8


def round_up(value, step):
    return -(-value // step) * step


def gelu_tanh(values):
    return jax.nn.gelu(values, approximate=True)


def body(
    lats, n, rows, cols, chans, pad, reach,
    x_hbm, metric_ref, k1_ref, k2_ref, widths_ref, gains_ref, gain_ref, win_hbm, wout_hbm,
    out_hbm,
    x_ref, first, weights, held, sec, acc, mix, circ, zsend, zrecv, out_ref,
    edge, edge_in, strip, strip_in, corner_in, near,
    taps, lines, taps_one, win_ref, wout_ref,
    w_sem, o_sem,
    hs_sem, hr_sem, fs_sem, fr_sem, rs_sem, rr_sem,
):
    lat = lax.axis_index("lat")
    me = lax.axis_index("lon")
    chunks = rows // n
    half = n // 2
    wide = LEAD + pad
    slabs = 2 * reach + 1
    pitch = first.shape[1] // wide
    step = held.shape[1] // pad
    tiles = [slice(c * LANES, (c + 1) * LANES) for c in range(chans // LANES)]

    at_top = lat == 0
    at_bottom = lat == lats - 1
    up_lat = jnp.where(at_top, 0, lat - 1)
    up_lon = jnp.where(at_top, lax.rem(me + half, n), me)
    down_lat = jnp.where(at_bottom, lats - 1, lat + 1)
    down_lon = jnp.where(at_bottom, lax.rem(me + half, n), me)
    left = lax.rem(me + n - 1, n)
    right = lax.rem(me + 1, n)

    def before(lon):
        return lax.rem(lon + n - 1, n)

    def after(lon):
        return lax.rem(lon + 1, n)

    x_load = pltpu.make_async_copy(x_hbm, x_ref, w_sem.at[2])
    x_load.start()
    loads = [
        pltpu.make_async_copy(win_hbm, win_ref, w_sem.at[0]),
        pltpu.make_async_copy(wout_hbm, wout_ref, w_sem.at[1]),
    ]
    for load in loads:
        load.start()

    barrier = pltpu.get_barrier_semaphore()
    greeted = [
        (lat, left), (lat, right),
        (up_lat, up_lon), (up_lat, before(up_lon)), (up_lat, after(up_lon)),
        (down_lat, down_lon), (down_lat, before(down_lon)), (down_lat, after(down_lon)),
    ] + [(lat, lax.rem(me + o, n)) for o in range(1, n)]
    for device in greeted:
        pl.semaphore_signal(barrier, inc=1, device_id=device, device_id_type=MESH)

    halo = []

    def send_halo(src, dst, recv_index, device):
        copy = pltpu.make_async_remote_copy(
            src_ref=src, dst_ref=dst, send_sem=hs_sem.at[len(halo)], recv_sem=hr_sem.at[recv_index],
            device_id=device, device_id_type=MESH,
        )
        copy.start()
        halo.append(copy)

    def recv_halo(src, dst, recv_index):
        pltpu.make_async_remote_copy(
            src_ref=src, dst_ref=dst, send_sem=hs_sem.at[0], recv_sem=hr_sem.at[recv_index],
            device_id=(lat, right), device_id_type=MESH,
        ).wait_recv()

    def spread(block, c):
        return jnp.broadcast_to(block[:, c:c + 1], (rows, LANES))

    def enter(c):
        weight = spread(metric_ref, c)
        at = (LEAD + c) * pitch + 2
        weights[at:at + rows] = weight
        for t, lanes in enumerate(tiles):
            cells = x_ref[c, :, lanes].astype(jnp.float32)
            held[t, c * step:c * step + rows] = cells
            value = (cells * weight).astype(jnp.bfloat16)
            first[t, at:at + rows] = value.astype(jnp.float32)
            if c < 2:
                strip[0, c, :, lanes] = value
            if c >= cols - 2:
                strip[1, c - cols + 2, :, lanes] = value

    rims = [0, 1, cols - 2, cols - 1]
    x_load.wait()
    for c in rims:
        enter(c)
    pl.semaphore_wait(barrier, len(greeted))

    up_side = jnp.where(at_top, 0, 1)
    down_side = jnp.where(at_bottom, 1, 0)
    for s, device in ((0, left), (1, right)):
        send_halo(strip.at[s], strip_in.at[1 - s], 4 + s, (lat, device))
        send_halo(metric_ref, near.at[1 - s], 10 + s, (lat, device))
    for side, src, device_lat, device_lon in (
        (up_side, 0, up_lat, up_lon), (down_side, rows - 8, down_lat, down_lon)
    ):
        send_halo(metric_ref, near.at[2 + side], 12 + side, (device_lat, device_lon))
        for s, lon in ((0, before(device_lon)), (1, after(device_lon))):
            send_halo(
                strip.at[s, :, pl.ds(src, 8)], corner_in.at[side, 1 - s], 6 + 2 * side + s, (device_lat, lon)
            )
            send_halo(metric_ref, near.at[4 + 2 * side + 1 - s], 14 + 2 * side + s, (device_lat, lon))

    for c in range(2, cols - 2):
        enter(c)
    for slot, row in enumerate((0, 1, rows - 2, rows - 1)):
        for t, lanes in enumerate(tiles):
            line = first[t, pl.ds(LEAD * pitch + row + 2, pad, stride=pitch), :]
            edge[slot, :, lanes] = line.astype(jnp.bfloat16)
    for i in range(2):
        up_slot = jnp.where(at_top, 1 - i, 2 + i)
        down_slot = jnp.where(at_bottom, 3 - i, i)
        send_halo(edge.at[i], edge_in.at[up_slot], up_slot, (up_lat, up_lon))
        send_halo(edge.at[2 + i], edge_in.at[down_slot], down_slot, (down_lat, down_lon))

    tap_lanes = taps.shape[2]
    lane_ids = lax.broadcasted_iota(jnp.int32, (pad, tap_lanes), 1)
    taps_one[0, 0:9] = k1_ref[...]
    for a in range(3):
        taps_one[1, 3 * a:3 * a + 3] = k1_ref[6 - 3 * a:9 - 3 * a, :]
    count = gains_ref.shape[1]
    center = (count - 1) // 2
    lines[...] = jnp.zeros(lines.shape, jnp.float32)
    lines[:, 0:count] = gains_ref[...].astype(jnp.float32)
    for k in range(chunks):
        line = jnp.broadcast_to(lines[pl.ds(k * n + me, 1), :], (pad, tap_lanes))
        kept = jnp.abs(lane_ids - center) <= widths_ref[k * n + me]
        line = jnp.where(kept, line, 0.0)
        shifted = pltpu.roll(line, 0, 1, stride=1, stride_axis=0)
        total = jnp.zeros((pad, tap_lanes), jnp.float32)
        for d in range(slabs):
            moved = pltpu.roll(shifted, (pad - cols) * d, 1) if d else shifted
            inside = (lane_ids >= pad * d) & (lane_ids < pad * d + cols)
            total = jnp.where(inside, moved, total)
        taps[k] = total.astype(jnp.bfloat16)

    for s in range(2):
        recv_halo(strip.at[s], strip_in.at[1 - s], 4 + s)
        recv_halo(metric_ref, near.at[1 - s], 10 + s)
    for s, start, c, from_col in ((0, LEAD - 2, LEAD - 1, cols - 1), (1, LEAD + cols, LEAD + cols, 0)):
        weights[c * pitch + 2:c * pitch + 2 + rows] = spread(near.at[s], from_col)
        for j in range(2):
            at = (start + j) * pitch + 2
            for t, lanes in enumerate(tiles):
                first[t, at:at + rows] = strip_in[s, j, :, lanes].astype(jnp.float32)

    def join_rows():
        for slot in range(4):
            recv_halo(edge.at[0], edge_in.at[slot], slot)
        for side in range(2):
            recv_halo(metric_ref, near.at[2 + side], 12 + side)
            for s in range(2):
                recv_halo(strip.at[s, :, pl.ds(0, 8)], corner_in.at[side, 1 - s], 6 + 2 * side + s)
                recv_halo(metric_ref, near.at[4 + 2 * side + 1 - s], 14 + 2 * side + s)
        diagonal = lax.broadcasted_iota(jnp.int32, (pad, cols), 0) == lax.broadcasted_iota(
            jnp.int32, (pad, cols), 1
        )
        for slot in range(4):
            row = slot if slot < 2 else rows + slot
            for t, lanes in enumerate(tiles):
                line = edge_in[slot, :, lanes].astype(jnp.float32)
                first[t, pl.ds(LEAD * pitch + row, cols, stride=pitch), :] = line[0:cols]
        for side, pole in ((0, at_top), (1, at_bottom)):
            lower = (rows - 1, 0)[side]
            source = jnp.where(pole, rows - 1 - lower, lower)
            row = (1, rows + 2)[side]
            line = jnp.broadcast_to(near[2 + side, pl.ds(source, 1), :], (pad, cols))
            column = jnp.sum(jnp.where(diagonal, line, 0.0), axis=1, keepdims=True)
            column = jnp.broadcast_to(column, (pad, LANES))
            weights[pl.ds(LEAD * pitch + row, cols, stride=pitch), :] = column[0:cols]
            for s, c, from_col in ((0, LEAD - 1, cols - 1), (1, LEAD + cols, 0)):
                cell = near[4 + 2 * side + s, pl.ds(source, 1), :]
                weights[c * pitch + row:c * pitch + row + 1] = jnp.broadcast_to(
                    cell[:, from_col:from_col + 1], (1, LANES)
                )
            top = (0, rows + 2)[side]
            for s, start in ((0, LEAD - 2), (1, LEAD + cols)):
                for j in range(2):
                    at = (start + j) * pitch + top
                    for t, lanes in enumerate(tiles):
                        cells = corner_in[side, s, j, :, lanes].astype(jnp.float32)
                        if side == 0:
                            plain, one, two = cells[6:8], cells[1:2], cells[0:1]
                        else:
                            plain, one, two = cells[0:2], cells[7:8], cells[6:7]
                        first[t, at:at + 1] = jnp.where(pole, one, plain[0:1])
                        first[t, at + 1:at + 2] = jnp.where(pole, two, plain[1:2])

    def stencil(load, kernel):
        sums = [None, None, None]
        for a in range(3):
            line = load(a)
            for b in range(3):
                term = kernel(a, b) * line
                sums[b] = term if sums[b] is None else sums[b] + term
        return pltpu.roll(sums[0], 1, 0) + sums[1] + pltpu.roll(sums[2], wide - 1, 0)

    def second_row(p, carry):
        flip = ((p == 0) & at_top) | ((p == rows + 1) & at_bottom)
        which = jnp.where(flip, 1, 0)
        weight = weights[pl.ds(p + 1, wide, stride=pitch), :]
        for t, lanes in enumerate(tiles):
            value = stencil(
                lambda a: first[t, pl.ds(p + a, wide, stride=pitch), :],
                lambda a, b: taps_one[which, 3 * a + b:3 * a + b + 1, lanes],
            )
            value = weight * gelu_tanh(value)
            sec[p, :, lanes] = value.astype(jnp.bfloat16).astype(jnp.float32)
        return carry

    col_ids = lax.broadcasted_iota(jnp.int32, (pad, LANES), 0)

    def mixed_row(i, carry):
        for t, lanes in enumerate(tiles):
            value = stencil(
                lambda a: sec[i + a, :, lanes],
                lambda a, b: k2_ref[3 * a + b:3 * a + b + 1, lanes],
            )
            value = held[t, pl.ds(i, pad, stride=step), :] + value[LEAD:, :]
            mix[i, :, lanes] = jnp.where(col_ids < cols, value, 0.0).astype(jnp.bfloat16)
        return carry

    forward = []
    order = list(range(1, chunks - 1)) + [0] + ([chunks - 1] if chunks > 1 else [])
    done = set()
    joined = False
    for k in order:
        if not joined and k in (0, chunks - 1):
            join_rows()
            joined = True
        needed = [p for p in range(k * n, (k + 1) * n + 2) if p not in done]
        done.update(needed)
        lax.fori_loop(needed[0], needed[-1] + 1, second_row, 0)
        lax.fori_loop(k * n, (k + 1) * n, mixed_row, 0)
        for o in range(1, n):
            target = lax.rem(me + o, n)
            copy = pltpu.make_async_remote_copy(
                src_ref=mix.at[k * n + target], dst_ref=circ.at[k, me + reach],
                send_sem=fs_sem.at[k, o], recv_sem=fr_sem.at[k, o],
                device_id=(lat, target), device_id_type=MESH,
            )
            copy.start()
            forward.append(copy)
        circ[k, me + reach] = mix[k * n + me]

    for copy in halo:
        copy.wait_send()
    for load in loads:
        load.wait()

    group = 8

    def network(g, carry):
        flat = mix[pl.ds(g * group, group)].reshape(group * pad, chans).astype(jnp.float32)
        scale = lax.rsqrt(jnp.mean(flat * flat, axis=1, keepdims=True) + 1e-06)
        normed = (flat * scale * gain_ref[...]).astype(jnp.bfloat16)
        hidden = gelu_tanh(
            jnp.dot(normed, win_ref[...], preferred_element_type=jnp.float32)
        ).astype(jnp.bfloat16)
        point = jnp.dot(hidden, wout_ref[...], preferred_element_type=jnp.float32)
        acc[pl.ds(g * group, group)] = (flat + point).reshape(group, pad, chans)
        return carry

    lax.fori_loop(0, rows // group, network, 0)

    back = []
    for k in order:
        for o in range(1, n):
            source = lax.rem(me + n - o, n)
            pltpu.make_async_remote_copy(
                src_ref=mix.at[k * n], dst_ref=circ.at[k, source + reach],
                send_sem=fs_sem.at[k, o], recv_sem=fr_sem.at[k, o],
                device_id=(lat, source), device_id_type=MESH,
            ).wait_recv()
        for e in range(reach):
            circ[k, e] = circ[k, n + e]
            circ[k, n + reach + e] = circ[k, reach + e]

        def filter_block(a, carry):
            window = circ[k, pl.ds(a, slabs)].reshape(slabs * pad, chans)
            result = jnp.dot(
                taps[k, :, 0:slabs * pad], window, preferred_element_type=jnp.float32
            )
            zsend[k * n + a] = result.astype(jnp.bfloat16)
            return carry

        lax.fori_loop(0, n, filter_block, 0, unroll=4)
        for o in range(1, n):
            target = lax.rem(me + o, n)
            copy = pltpu.make_async_remote_copy(
                src_ref=zsend.at[k * n + target], dst_ref=zrecv.at[k * n + me],
                send_sem=rs_sem.at[k, o], recv_sem=rr_sem.at[k, o],
                device_id=(lat, target), device_id_type=MESH,
            )
            copy.start()
            back.append(copy)
        zrecv[k * n + me] = zsend[k * n + me]

    stores = []
    for k in order:
        for o in range(1, n):
            source = lax.rem(me + n - o, n)
            pltpu.make_async_remote_copy(
                src_ref=zsend.at[k * n], dst_ref=zrecv.at[k * n + source],
                send_sem=rs_sem.at[k, o], recv_sem=rr_sem.at[k, o],
                device_id=(lat, source), device_id_type=MESH,
            ).wait_recv()

        def finish(i, carry):
            for t, lanes in enumerate(tiles):
                value = acc[i, :, lanes] + zrecv[i, :, lanes].astype(jnp.float32)
                held[t, pl.ds(i, cols, stride=step), :] = value[0:cols]
            return carry

        lax.fori_loop(k * n, (k + 1) * n, finish, 0)
        for c in range(cols):
            for t, lanes in enumerate(tiles):
                at = c * step + k * n
                out_ref[c, k * n:(k + 1) * n, lanes] = held[t, at:at + n].astype(jnp.bfloat16)
        store = pltpu.make_async_copy(
            out_ref.at[:, pl.ds(k * n, n)], out_hbm.at[:, pl.ds(k * n, n)], o_sem.at[k]
        )
        store.start()
        stores.append(store)

    for copy in forward + back:
        copy.wait_send()
    for store in stores:
        store.wait()


def local(
    lats, n,
    inputs, metric, kernel_one, kernel_two, widths, zonal_gains, norm_gain, weight_in, weight_out
):
    rows, cols, chans = inputs.shape
    pad = round_up(cols, 16)
    wide = LEAD + pad
    reach = n // 4
    slabs = 2 * reach + 1
    count = zonal_gains.shape[1]
    tap_lanes = round_up(max(slabs * pad, count + pad - 1), LANES)
    pitch = (rows + 4) | 1
    step = rows | 1

    chunks = rows // n
    tiles = chans // LANES
    vmem = pl.BlockSpec(memory_space=pltpu.VMEM)
    hbm = pl.BlockSpec(memory_space=pl.ANY)
    sem = pltpu.SemaphoreType.DMA
    out = pl.pallas_call(
        functools.partial(body, lats, n, rows, cols, chans, pad, reach),
        out_shape=jax.ShapeDtypeStruct((cols, rows, chans), jnp.bfloat16),
        in_specs=[hbm] + [vmem] * 3
        + [pl.BlockSpec(memory_space=pltpu.SMEM), vmem, vmem]
        + [hbm] * 2,
        out_specs=hbm,
        scratch_shapes=[
            pltpu.VMEM((cols, rows, chans), jnp.bfloat16),
            pltpu.VMEM((tiles, wide * pitch, LANES), jnp.float32),
            pltpu.VMEM((wide * pitch, LANES), jnp.float32),
            pltpu.VMEM((tiles, pad * step, LANES), jnp.float32),
            pltpu.VMEM((rows + 2, wide, chans), jnp.float32),
            pltpu.VMEM((rows, pad, chans), jnp.float32),
            pltpu.VMEM((rows, pad, chans), jnp.bfloat16),
            pltpu.VMEM((chunks, n + 2 * reach, pad, chans), jnp.bfloat16),
            pltpu.VMEM((rows, pad, chans), jnp.bfloat16),
            pltpu.VMEM((rows, pad, chans), jnp.bfloat16),
            pltpu.VMEM((cols, rows, chans), jnp.bfloat16),
            pltpu.VMEM((4, pad, chans), jnp.bfloat16),
            pltpu.VMEM((4, pad, chans), jnp.bfloat16),
            pltpu.VMEM((2, 2, rows, chans), jnp.bfloat16),
            pltpu.VMEM((2, 2, rows, chans), jnp.bfloat16),
            pltpu.VMEM((2, 2, 2, 8, chans), jnp.bfloat16),
            pltpu.VMEM((8, rows, cols), jnp.float32),
            pltpu.VMEM((chunks, pad, tap_lanes), jnp.bfloat16),
            pltpu.VMEM((rows, tap_lanes), jnp.float32),
            pltpu.VMEM((2, 16, chans), jnp.float32),
            pltpu.VMEM(weight_in.shape, jnp.bfloat16),
            pltpu.VMEM(weight_out.shape, jnp.bfloat16),
            sem((3,)), sem((chunks,)),
            sem((18,)), sem((18,)),
            sem((chunks, n)), sem((chunks, n)), sem((chunks, n)), sem((chunks, n)),
        ],
        compiler_params=pltpu.CompilerParams(
            collective_id=0, has_side_effects=True, vmem_limit_bytes=60 * 2**20
        ),
    )(
        inputs.transpose(1, 0, 2), metric, kernel_one, kernel_two, widths, zonal_gains, norm_gain.reshape(1, chans),
        weight_in, weight_out,
    )
    return out.transpose(1, 0, 2)


def solution(mesh):
    placed = (
        P("lat", "lon", None),
        P("lat", "lon"),
        P(),
        P(),
        P("lat"),
        P("lat", None),
        P(),
        P(),
        P(),
    )
    return jax.shard_map(
        functools.partial(local, mesh.shape["lat"], mesh.shape["lon"]),
        mesh=mesh, in_specs=placed, out_specs=P("lat", "lon", None), check_vma=False,
    )
```

time: 58 us -> 52.4 us (0.903)
  Pallas kernels: 54.5 us -> 49.5 us
  local copies, waits for them, and re-layouts: 3.35 us -> 2.65 us
    pallas_call x1, Pallas kernels: 54.5 us -> 49.5 us  [local(): pl.pallas_call(functools.partial(body, lats, n, rows, cols, chans, pad, r...]
    slice x1 -> x0, local copies, waits for them, and re-layouts: 3.35 us -> none  [local(): return out[:, :cols]]
    unnamed x0 -> x1, local copies, waits for them, and re-layouts: none -> 2.65 us
where the time goes in v1:
time: 52.4 us; the launch traced here: 52.2 us
  Pallas kernels  49.5 us (94%)
  local copies, waits for them, and re-layouts  2.65 us (5%)
    pallas_call x1, Pallas kernels, local(): pl.pallas_call(functools.partial(body, lats, n, rows, cols, chans, pad, r...  49.5 us
    unnamed x1, local copies, waits for them, and re-layouts  2.65 us

profile of v1, /device:TPU:0, one launch (start us, length us, event | category | flops | bytes accessed | tf_op | source)
XLA Modules:
  0.0 52.2 jit_solution(18421966077826357619)
XLA Ops:
  0.0 49.5 %shard_map.91 = bf16[45,32,512]{2,1,0:T(8,128)(2,1)} custom-call(bf16[45,32,512]{2,1,0:T(8,128)(2,1)} %bitcast.4, f32[32,45]{1,0:T(8,128)} %metric_ref.1, f32[9,512]{1,0:T(8,128)} %k1_ref.1, f32[9,512]{1,0:T(8,128)} %k2_ref.1, s32[32]{0:T(128)} %widths_ref.1, bf16[32,181]{1,0:T(8,128)(2,1)} %gains_ref.1, f32[1,512]{1,0:T(1,128)} %bitcast.5, ...), custom_call_target="tpu_custom_call" | custom-call | tf_op jit(solution)/shard_map/pallas_call | solution.py:377
  49.6 2.7 %copy.11 = bf16[32,45,512]{2,0,1:T(8,128)(2,1)} copy(bf16[32,45,512]{2,0,1:T(8,128)(2,1)} %bitcast.3) | data formatting | bytes 2949120

commit v2 on v1

--- a/solution.py
+++ b/solution.py
@@ -307,34 +307,34 @@
             result = jnp.dot(
                 taps[k, :, 0:slabs * pad], window, preferred_element_type=jnp.float32
             )
-            zsend[k * n + a] = result.astype(jnp.bfloat16)
+            zsend[a * chunks + k] = result.astype(jnp.bfloat16)
             return carry
 
         lax.fori_loop(0, n, filter_block, 0, unroll=4)
         for o in range(1, n):
             target = lax.rem(me + o, n)
             copy = pltpu.make_async_remote_copy(
-                src_ref=zsend.at[k * n + target], dst_ref=zrecv.at[k * n + me],
+                src_ref=zsend.at[target * chunks + k], dst_ref=zrecv.at[me * chunks + k],
                 send_sem=rs_sem.at[k, o], recv_sem=rr_sem.at[k, o],
                 device_id=(lat, target), device_id_type=MESH,
             )
             copy.start()
             back.append(copy)
-        zrecv[k * n + me] = zsend[k * n + me]
+        zrecv[me * chunks + k] = zsend[me * chunks + k]
 
     stores = []
     for k in order:
         for o in range(1, n):
             source = lax.rem(me + n - o, n)
             pltpu.make_async_remote_copy(
-                src_ref=zsend.at[k * n], dst_ref=zrecv.at[k * n + source],
+                src_ref=zsend.at[k], dst_ref=zrecv.at[source * chunks + k],
                 send_sem=rs_sem.at[k, o], recv_sem=rr_sem.at[k, o],
                 device_id=(lat, source), device_id_type=MESH,
             ).wait_recv()
 
         def finish(i, carry):
             for t, lanes in enumerate(tiles):
-                value = acc[i, :, lanes] + zrecv[i, :, lanes].astype(jnp.float32)
+                value = acc[i, :, lanes] + zrecv[(i - k * n) * chunks + k, :, lanes].astype(jnp.float32)
                 held[t, pl.ds(i, cols, stride=step), :] = value[0:cols]
             return carry
 

time: 52.4 us -> 52.4 us (level)
  no operation moved by 1% of the time
where the time goes in v2:
time: 52.4 us; the launch traced here: 52.2 us
  Pallas kernels  49.5 us (94%)
  local copies, waits for them, and re-layouts  2.65 us (5%)
    pallas_call x1, Pallas kernels, local(): pl.pallas_call(functools.partial(body, lats, n, rows, cols, chans, pad, r...  49.5 us
    unnamed x1, local copies, waits for them, and re-layouts  2.65 us

profile of v2, /device:TPU:0, one launch (start us, length us, event | category | flops | bytes accessed | tf_op | source)
XLA Modules:
  0.0 52.2 jit_solution(14711132548662520381)
XLA Ops:
  0.0 49.5 %shard_map.91 = bf16[45,32,512]{2,1,0:T(8,128)(2,1)} custom-call(bf16[45,32,512]{2,1,0:T(8,128)(2,1)} %bitcast.4, f32[32,45]{1,0:T(8,128)} %metric_ref.1, f32[9,512]{1,0:T(8,128)} %k1_ref.1, f32[9,512]{1,0:T(8,128)} %k2_ref.1, s32[32]{0:T(128)} %widths_ref.1, bf16[32,181]{1,0:T(8,128)(2,1)} %gains_ref.1, f32[1,512]{1,0:T(1,128)} %bitcast.5, ...), custom_call_target="tpu_custom_call" | custom-call | tf_op jit(solution)/shard_map/pallas_call | solution.py:377
  49.6 2.7 %copy.11 = bf16[32,45,512]{2,0,1:T(8,128)(2,1)} copy(bf16[32,45,512]{2,0,1:T(8,128)(2,1)} %bitcast.3) | data formatting | bytes 2949120
